TPU v7x, 128 devices: a whole 4x4x4 slice. The times are simulated.
128 devices in a mesh: sec: 4 (over y_hi, core), dev: 32 (over z, y_lo, x).
Axes of the slice: x: 4, y: 4 (y_hi: 2, y_lo: 2; y = y_hi * 2 + y_lo), z: 4, core: 2. Of those that a mesh axis runs over, the one named last changes fastest.
Arguments:
- queries: bfloat16 [256, 8192], P('dev', 'sec')
- fresh_key_value: bfloat16 [2, 256, 512], P(None, 'dev', 'sec'), may hold values from -6 to 6
- key_value_cache: bfloat16 [2, 256, 1024, 512], P(None, 'dev', None, 'sec'), may hold values from -6 to 6
- lengths: int32 [256], P('dev'), may hold values from 1 to 1024, as said below
- residual: bfloat16 [256, 4096], P(None, 'dev'), may hold values from -6 to 6
- out_weight: bfloat16 [8192, 4096], P('sec', 'dev'), may hold values from -0.0625 to 0.0625
- norm_gain: float32 [4096], P('dev'), may hold values from 0.1 to 1.9
- routes: int32 [256, 8], replicated, may hold values from 0 to 63, all different within a row; in each aligned block of 256 rows (0 to 255, 256 to 511, ...) at most 64 rows name the same one
- route_weights: float32 [256, 8], replicated, may hold values from 0.05 to 0.5
- w_gate: bfloat16 [64, 4096, 1536], P('dev', None, 'sec'), may hold values from -0.09375 to 0.09375
- w_up: bfloat16 [64, 4096, 1536], P('dev', None, 'sec'), may hold values from -0.09375 to 0.09375
- w_down: bfloat16 [64, 1536, 4096], P('dev', 'sec'), may hold values from -0.15625 to 0.15625
Outputs:
- layer_out: bfloat16 [256, 4096], P(None, 'dev')
Inputs may be any that keep to these rules, and one draw needn't show every extreme that they name: `routes`: each row names 8 different experts; no expert is named by more than 64 rows, a bound that some block reaches. `lengths`: some row has all 1024 slots filled.
All inputs are finite; a program needn't handle non-finite values.
Results may differ from a plain program's by a relative error of at most 0.0055.
Values may be sent and summed in bfloat16 or wider, within the bound.
No kernel may reach another device: no remote copies, remote signals or barrier semaphores. Data moves between devices by JAX's collectives and lax.ppermute only.
A program may use at most 128 MiB of HBM per device.

v0:
```python
import math
import jax
import jax.numpy as jnp
from jax import lax
from jax.sharding import PartitionSpec as P

D = 4096
QUERY_HEADS = 64
KEY_VALUE_HEADS = 4
HEAD_SIZE = 128
CAP = 64


def attend(queries, fresh_key_value, key_value_cache, lengths):
    row_count = key_value_cache.shape[1]
    cache_length = key_value_cache.shape[2]
    heads_kv = key_value_cache.shape[3] // HEAD_SIZE
    queries_per_group = QUERY_HEADS // KEY_VALUE_HEADS
    score_scale = 1.0 / math.sqrt(HEAD_SIZE)
    head_queries = queries.reshape(row_count, heads_kv, queries_per_group, HEAD_SIZE)
    cached_keys = key_value_cache[0].reshape(row_count, cache_length, heads_kv, HEAD_SIZE)
    cached_values = key_value_cache[1].reshape(row_count, cache_length, heads_kv, HEAD_SIZE)
    own_key = fresh_key_value[0].reshape(row_count, heads_kv, HEAD_SIZE)
    own_value = fresh_key_value[1].reshape(row_count, heads_kv, HEAD_SIZE).astype(jnp.float32)
    scores = (
        jnp.einsum("rkgd,rtkd->rkgt", head_queries, cached_keys, preferred_element_type=jnp.float32)
        * score_scale
    )
    own_score = (
        jnp.einsum("rkgd,rkd->rkg", head_queries, own_key, preferred_element_type=jnp.float32)
        * score_scale
    )
    visible = (jnp.arange(cache_length, dtype=jnp.int32)[None, :] < lengths[:, None])[
        :, None, None, :
    ]
    row_max = jnp.maximum(jnp.max(jnp.where(visible, scores, -jnp.inf), axis=-1), own_score)
    weights = jnp.where(visible, jnp.exp(scores - row_max[..., None]), 0.0)
    own_weight = jnp.exp(own_score - row_max)
    normalizer = jnp.sum(weights, axis=-1) + own_weight
    weighted = jnp.einsum(
        "rkgt,rtkd->rkgd",
        weights.astype(jnp.bfloat16),
        cached_values,
        preferred_element_type=jnp.float32,
    )
    weighted = weighted + own_weight[..., None] * own_value[:, :, None, :]
    return (
        (weighted / normalizer[..., None])
        .astype(jnp.bfloat16)
        .reshape(row_count, heads_kv * queries_per_group * HEAD_SIZE)
    )


def slot_layout(routes, route_weights, expert_ids):
    matches = routes[:, :, None] == expert_ids[None, None, :]
    chosen = jnp.any(matches, axis=1)
    shares = jnp.sum(jnp.where(matches, route_weights[:, :, None], 0.0), axis=1)
    slot_rank = jnp.cumsum(chosen.astype(jnp.int32), axis=0, dtype=jnp.int32) - 1
    slot_ids = jnp.arange(CAP, dtype=jnp.int32)
    slot_mask = (chosen[:, :, None] & (slot_rank[:, :, None] == slot_ids[None, None, :])).transpose(
        1, 2, 0
    )
    spread = slot_mask.astype(jnp.float32) * shares.T[:, None, :]
    return (slot_mask, spread)


def expert_results(full_rows, slot_mask, w_gate, w_up, w_down):
    picked = jnp.einsum(
        "ecr,rd->ecd", slot_mask.astype(jnp.bfloat16), full_rows, preferred_element_type=jnp.float32
    ).astype(jnp.bfloat16)
    gate_part = jnp.einsum("ecd,edf->ecf", picked, w_gate, preferred_element_type=jnp.float32)
    upward = jnp.einsum("ecd,edf->ecf", picked, w_up, preferred_element_type=jnp.float32)
    activation = (jax.nn.silu(gate_part) * upward).astype(jnp.bfloat16)
    return jnp.einsum("ecf,efd->ecd", activation, w_down, preferred_element_type=jnp.float32)


def shards(
    queries,
    fresh_key_value,
    key_value_cache,
    lengths,
    residual,
    out_weight,
    norm_gain,
    routes,
    route_weights,
    w_gate,
    w_up,
    w_down,
):
    attn = attend(queries, fresh_key_value, key_value_cache, lengths)
    partial_out = jnp.dot(
        lax.all_gather(attn, "dev", axis=0, tiled=True),
        out_weight,
        preferred_element_type=jnp.float32,
    )
    hidden = residual.astype(jnp.float32) + lax.psum(partial_out, "sec")
    square_sum = lax.psum(jnp.sum(hidden * hidden, axis=-1, keepdims=True), "dev")
    normed = (hidden * lax.rsqrt(square_sum / D + 1e-06) * norm_gain).astype(jnp.bfloat16)
    full_rows = lax.all_gather(normed, "dev", axis=1, tiled=True)
    local_count = w_gate.shape[0]
    local_ids = lax.axis_index("dev") * local_count + jnp.arange(local_count, dtype=jnp.int32)
    slot_mask, spread = slot_layout(routes, route_weights, local_ids)
    result = expert_results(full_rows, slot_mask, w_gate, w_up, w_down)
    expert_term = jnp.einsum("ecr,ecd->rd", spread, result, precision=lax.Precision.HIGHEST)
    mixture = lax.psum(lax.psum_scatter(expert_term, "dev", scatter_dimension=1, tiled=True), "sec")
    return (hidden + mixture).astype(jnp.bfloat16)


def solution(mesh):
    return jax.shard_map(
        shards,
        mesh=mesh,
        in_specs=(
            P("dev", "sec"),
            P(None, "dev", "sec"),
            P(None, "dev", None, "sec"),
            P("dev"),
            P(None, "dev"),
            P("sec", "dev"),
            P("dev"),
            P(),
            P(),
            P("dev", None, "sec"),
            P("dev", None, "sec"),
            P("dev", "sec", None),
        ),
        out_specs=P(None, "dev"),
        check_vma=False,
    )
```

profile of v0, /device:TPU:1, one launch (start us, length us, event | category | flops | bytes accessed | tf_op | source)
XLA Modules:
  0.0 653.0 jit_solution(15178874167412993256)
XLA Ops:
  6.5 0.0 copy-start
  6.5 0.0 copy-start.2
  6.5 0.0 all-gather.3.cloned.1.call-start
  6.5 0.8 bitcast_convert_fusion
  7.3 0.7 iota_compare_fusion.1
  8.0 0.9 fusion.46
  8.9 0.0 copy-start.5
  8.9 0.0 copy-start.3
  8.9 0.0 copy-start.4
  8.9 2.4 select_reduce_fusion
  11.3 0.2 fusion.24
  11.6 2.1 fusion.21
  13.7 0.6 copy.34
  14.3 0.0 all-gather.3.cloned.1.call-update
  14.3 0.0 all-reduce.3.cloned.1.call-start
  14.4 132.9 %all-gather.3.cloned.1.call-done = bf16[256,2048]{1,0:T(8,128)(2,1)} async-done(((bf16[8,2048]{1,0:T(8,128)(2,1)}), bf16[256,2048]{1,0:T(8,128)(2,1)}) %all-gather.3.cloned.1.call-update) | async-done | bytes 1048592 | tf_op jit(solution)/shard_map/all_gather | solution.py:93
  147.2 0.0 copy-done
  147.2 2.3 fusion.55
  149.5 0.0 all-reduce.3.cloned.1.call-update
  149.5 0.0 all-gather.5.cloned.1.call-start
  149.6 62.2 %all-reduce.3.cloned.1.call-done = f32[256,128]{1,0:T(8,128)} async-done(((f32[256,128]{1,0:T(8,128)}), f32[256,128]{1,0:T(8,128)}) %all-reduce.3.cloned.1.call-update) | async-done | bytes 131088 | tf_op jit(solution)/shard_map/psum | solution.py:97
  211.8 0.0 copy-done.2
  211.8 1.0 multiply_reduce_fusion
  212.9 68.0 %psum.22 = f32[256,1]{0,1:T(1,128)S(1)} all-reduce(f32[256,1]{0,1:T(1,128)S(1)} %bitcast.67), channel_id=1, replica_groups=mesh['sec'=4,'dev'=32] {'dev'}, use_global_device_ids=true, to_apply=%region_8.9 | all-reduce | flops 256 | bytes 2048 | tf_op jit(solution)/shard_map/psum | solution.py:98
  280.9 0.0 copy-done.5
  280.9 1.6 multiply_convert_fusion
  282.5 0.0 all-gather.5.cloned.1.call-update
  282.6 0.0 reduce-scatter.2.cloned.1.call-start
  282.6 0.0 copy-done.3
  282.6 0.1 compare_reduce_fusion
  282.7 0.6 reduce-window.6
  283.4 0.2 slice_reduce_fusion
  283.6 0.2 reduce-window.9
  283.7 0.1 add_bitcast_fusion
  283.8 0.0 copy-done.4
  283.8 0.1 fusion.49
  283.9 116.7 %all-gather.5.cloned.1.call-done = bf16[256,4096]{1,0:T(8,128)(2,1)} async-done(((bf16[256,128]{1,0:T(8,128)(2,1)}), bf16[256,4096]{1,0:T(8,128)(2,1)}) %all-gather.5.cloned.1.call-update) | async-done | bytes 2097168 | tf_op jit(solution)/shard_map/all_gather | solution.py:100
  400.6 2.0 convolution_convert_fusion
  402.6 3.8 fusion.56
  406.4 8.1 %fusion.11 = f32[2,64,4096]{2,1,0:T(8,128)} fusion(bf16[2,384,4096]{2,1,0:T(8,128)(2,1)} %param.23, bf16[2,64,4096]{2,1,0:T(8,128)(2,1)S(1)} %convolution_convert_fusion, bf16[2,4096,384]{2,1,0:T(8,128)(2,1)} %param.22, f32[2,64,384]{2,1,0:T(8,128)S(1)} %fusion.56), kind=kOutput, calls=%fused_computation.12 | convolution fusion | flops 805601280 | bytes 15925248 | tf_op jit(solution)/shard_map/ecf,efd->ecd/dot_general | solution.py:74
  414.5 0.0 copy-start.1
  414.5 6.8 %convolution_bitcast_fusion = f32[256,4096]{1,0:T(8,128)} fusion(f32[2,64,4096]{2,1,0:T(8,128)} %fusion.11, f32[2,256]{1,0:T(2,128)S(1)} %bitcast.65, s32[2,256]{1,0:T(2,128)S(1)} %bitcast.58, pred[2,256]{1,0:T(4,128)(4,1)S(1)} %bitcast.62), kind=kOutput, calls=%fused_computation | convolution fusion | flops 1610711040 | bytes 6296064 | tf_op jit(solution)/shard_map/ecr,ecd->rd/dot_general | solution.py:105
  421.3 0.0 reduce-scatter.2.cloned.1.call-update
  421.3 0.0 all-reduce.5.cloned.1.call-start
  421.4 162.3 %reduce-scatter.2.cloned.1.call-done = f32[256,128]{1,0:T(8,128)} async-done(((f32[256,4096]{1,0:T(8,128)}), f32[256,128]{1,0:T(8,128)}) %reduce-scatter.2.cloned.1.call-update) | async-done | bytes 131088 | tf_op jit(solution)/shard_map/reduce_scatter | solution.py:106
  583.7 0.0 all-reduce.5.cloned.1.call-update
  583.7 61.2 %all-reduce.5.cloned.1.call-done = f32[256,128]{1,0:T(8,128)} async-done(((f32[256,128]{1,0:T(8,128)}), f32[256,128]{1,0:T(8,128)}) %all-reduce.5.cloned.1.call-update) | async-done | bytes 131088 | tf_op jit(solution)/shard_map/psum | solution.py:106
  645.0 0.0 copy-done.1
  645.0 1.6 add_convert_fusion
  (7 shorter events, 0.1 us)
Async XLA Ops:
  6.5 140.7 %copy-start = (bf16[2048,128]{1,0:T(8,128)(2,1)S(1)}, bf16[2048,128]{1,0:T(8,128)(2,1)}, u32[]{:S(2)}) copy-start(bf16[2048,128]{1,0:T(8,128)(2,1)} %param.17) | copy-start | bytes 1572868
  6.5 205.3 %copy-start.2 = (bf16[256,128]{1,0:T(8,128)(2,1)S(1)}, bf16[256,128]{1,0:T(8,128)(2,1)}, u32[]{:S(2)}) copy-start(bf16[256,128]{1,0:T(8,128)(2,1)} %param.16) | copy-start | bytes 196612
  6.5 140.7 %all-gather.3.cloned.1.call-start = ((), (), s32[]{:S(2)}) async-start(), calls=%async_computation.1 | async-start | bytes 1081344 | tf_op jit(solution)/shard_map/all_gather | solution.py:93
  8.9 272.0 %copy-start.5 = (f32[128]{0:T(128)S(1)}, f32[128]{0:T(128)}, u32[]{:S(2)}) copy-start(f32[128]{0:T(128)} %param.18) | copy-start | bytes 1540
  8.9 273.7 %copy-start.3 = (s32[256,8]{0,1:T(8,128)S(1)}, s32[256,8]{0,1:T(8,128)}, u32[]{:S(2)}) copy-start(s32[256,8]{0,1:T(8,128)} %param.19) | copy-start | bytes 24580
  8.9 274.9 %copy-start.4 = (f32[256,8]{0,1:T(8,128)S(1)}, f32[256,8]{0,1:T(8,128)}, u32[]{:S(2)}) copy-start(f32[256,8]{0,1:T(8,128)} %param.20) | copy-start | bytes 24580
  14.3 197.5 %all-reduce.3.cloned.1.call-start = ((), (), s32[]{:S(2)}) async-start(), calls=%async_computation.2 | async-start | bytes 262144 | tf_op jit(solution)/shard_map/psum | solution.py:97
  149.5 251.0 %all-gather.5.cloned.1.call-start = ((), (), s32[]{:S(2)}) async-start(), calls=%async_computation.3 | async-start | bytes 2162688 | tf_op jit(solution)/shard_map/all_gather | solution.py:100
  282.6 301.2 %reduce-scatter.2.cloned.1.call-start = ((), (), s32[]{:S(2)}) async-start(), calls=%async_computation.4 | async-start | bytes 4325376 | tf_op jit(solution)/shard_map/reduce_scatter | solution.py:106
  414.5 230.4 %copy-start.1 = (f32[256,128]{1,0:T(8,128)S(1)}, f32[256,128]{1,0:T(8,128)}, u32[]{:S(2)}) copy-start(f32[256,128]{1,0:T(8,128)} %all-reduce.3.cloned.1.call-done) | copy-start | bytes 393220
  421.3 223.6 %all-reduce.5.cloned.1.call-start = ((), (), s32[]{:S(2)}) async-start(), calls=%async_computation.5 | async-start | bytes 262144 | tf_op jit(solution)/shard_map/psum | solution.py:106
Sparse Core Ops, SparseCore 0:
  14.4 132.7 all-gather.2
  149.7 62.0 all-reduce.2
  282.7 117.8 all-gather.4
  421.4 162.2 reduce-scatter.1
  586.2 58.7 all-reduce.4
where the time goes:
time: 654 us; the launch traced here: 653 us
  waiting for transfers between devices  535 us (82%)
  blocking collectives  68 us (10%)
  matrix products  28.3 us (4%)
  between operations  13.2 us (2%)
  other arithmetic  7.04 us (1%)
    reduce_scatter x1, waiting for transfers between devices, shards(): lax.psum_scatter(expert_term, 'dev', scatter_dimension=1, tiled=True)  162 us
    all_gather x1, waiting for transfers between devices, shards(): lax.all_gather(attn, 'dev', axis=0, tiled=True)  133 us
    all_gather x1, waiting for transfers between devices, shards(): full_rows = lax.all_gather(normed, 'dev', axis=1, tiled=True)  117 us
    psum x1, blocking collectives, shards(): lax.psum(jnp.sum(hidden * hidden, axis=-1, keepdims=True), 'dev')  68 us
    psum x1, waiting for transfers between devices, shards(): hidden = residual.astype(jnp.float32) + lax.psum(partial_out, 'sec')  62.2 us
    psum x1, waiting for transfers between devices, shards(): lax.psum(lax.psum_scatter(expert_term, 'dev', scatter_dimension=1, tiled=...  61.2 us
  transfers between devices with their start and end apart: 5, of which 5 were waited for; matrix products, arithmetic and copies ran while one was open for 0% of the time, Pallas kernels for 0%

commit v1 on v0

--- a/solution.py
+++ b/solution.py
@@ -90,7 +90,9 @@
 ):
     attn = attend(queries, fresh_key_value, key_value_cache, lengths)
     partial_out = jnp.dot(
-        lax.all_gather(attn, "dev", axis=0, tiled=True),
+        jnp.concatenate(
+            lax.all_to_all(jnp.stack([attn] * lax.axis_size("dev")), "dev", 0, 0), axis=0
+        ),
         out_weight,
         preferred_element_type=jnp.float32,
     )

time: 654 us -> 523 us (0.80)
  waiting for transfers between devices: 535 us -> 381 us
  blocking collectives: 68 us -> 93 us
    all_gather x1 -> x0, waiting for transfers between devices: 133 us -> none  [shards(): lax.all_gather(attn, 'dev', axis=0, tiled=True)]
    all_to_all x0 -> x1, blocking collectives: none -> 24.9 us  [shards(): lax.all_to_all(jnp.stack([attn] * lax.axis_size('dev')), 'dev', 0, 0)]
    psum x1, waiting for transfers between devices: 62.2 us -> 40.9 us  [shards(): hidden = residual.astype(jnp.float32) + lax.psum(partial_out, 'sec')]
  transfers between devices with their start and end apart: 5 -> 4, of which waited for: 5 -> 4; matrix products, arithmetic and copies ran while one was open for 0% -> 0% of each run, Pallas kernels for 0% -> 0%
where the time goes in v1:
time: 523 us; the launch traced here: 522 us
  waiting for transfers between devices  381 us (73%)
  blocking collectives  93 us (18%)
  matrix products  27.1 us (5%)
  between operations  13.2 us (3%)
  other arithmetic  7.03 us (1%)
    reduce_scatter x1, waiting for transfers between devices, shards(): lax.psum_scatter(expert_term, 'dev', scatter_dimension=1, tiled=True)  161 us
    all_gather x1, waiting for transfers between devices, shards(): full_rows = lax.all_gather(normed, 'dev', axis=1, tiled=True)  117 us
    psum x1, blocking collectives, shards(): lax.psum(jnp.sum(hidden * hidden, axis=-1, keepdims=True), 'dev')  68 us
    psum x1, waiting for transfers between devices, shards(): lax.psum(lax.psum_scatter(expert_term, 'dev', scatter_dimension=1, tiled=...  62.3 us
    psum x1, waiting for transfers between devices, shards(): hidden = residual.astype(jnp.float32) + lax.psum(partial_out, 'sec')  40.9 us
    all_to_all x1, blocking collectives, shards(): lax.all_to_all(jnp.stack([attn] * lax.axis_size('dev')), 'dev', 0, 0)  24.9 us
  transfers between devices with their start and end apart: 4, of which 4 were waited for; matrix products, arithmetic and copies ran while one was open for 0% of the time, Pallas kernels for 0%

profile of v1, /device:TPU:1, one launch (start us, length us, event | category | flops | bytes accessed | tf_op | source)
XLA Modules:
  0.0 522.1 jit_solution(13304548301635612657)
XLA Ops:
  6.5 0.0 copy-start
  6.5 0.0 all-reduce.3.cloned.1.call-start
  6.5 0.8 bitcast_convert_fusion
  7.3 0.7 iota_compare_fusion.1
  8.0 0.9 fusion.48
  8.9 2.4 select_reduce_fusion
  11.3 0.2 fusion.26
  11.5 0.0 copy-start.2
  11.5 0.0 copy-start.5
  11.6 0.0 copy-start.3
  11.6 0.0 copy-start.4
  11.6 2.1 fusion.21
  13.7 0.1 stack.3
  13.8 24.9 %all_to_all.5 = bf16[32,8,2048]{2,1,0:T(8,128)(2,1)S(1)} all-to-all(bf16[32,8,2048]{2,1,0:T(8,128)(2,1)S(1)} %stack.3), channel_id=1, replica_groups=mesh['sec'=4,'dev'=32] {'dev'}, dimensions={0} | all-to-all | bytes 2097152 | tf_op jit(solution)/shard_map/all_to_all | solution.py:94
  38.8 0.0 copy-done
  38.8 1.1 fusion.24
  39.8 0.0 all-reduce.3.cloned.1.call-update
  39.9 0.0 all-gather.2.cloned.1.call-start
  39.9 40.9 %all-reduce.3.cloned.1.call-done = f32[256,128]{1,0:T(8,128)} async-done(((f32[256,128]{1,0:T(8,128)}), f32[256,128]{1,0:T(8,128)}) %all-reduce.3.cloned.1.call-update) | async-done | bytes 131088 | tf_op jit(solution)/shard_map/psum | solution.py:99
  80.8 0.0 copy-done.2
  80.8 1.0 multiply_reduce_fusion
  81.8 68.0 %psum.22 = f32[256,1]{0,1:T(1,128)S(1)} all-reduce(f32[256,1]{0,1:T(1,128)S(1)} %bitcast.69), channel_id=1, replica_groups=mesh['sec'=4,'dev'=32] {'dev'}, use_global_device_ids=true, to_apply=%region_8.9 | all-reduce | flops 256 | bytes 2048 | tf_op jit(solution)/shard_map/psum | solution.py:100
  149.8 0.0 copy-done.5
  149.8 1.6 multiply_convert_fusion
  151.5 0.0 all-gather.2.cloned.1.call-update
  151.5 0.0 reduce-scatter.2.cloned.1.call-start
  151.6 0.0 copy-done.3
  151.6 0.1 compare_reduce_fusion
  151.7 0.6 reduce-window.6
  152.3 0.2 slice_reduce_fusion
  152.5 0.2 reduce-window.9
  152.7 0.1 add_bitcast_fusion
  152.8 0.0 copy-done.4
  152.8 0.1 fusion.51
  152.9 116.7 %all-gather.2.cloned.1.call-done = bf16[256,4096]{1,0:T(8,128)(2,1)} async-done(((bf16[256,128]{1,0:T(8,128)(2,1)}), bf16[256,4096]{1,0:T(8,128)(2,1)}) %all-gather.2.cloned.1.call-update) | async-done | bytes 2097168 | tf_op jit(solution)/shard_map/all_gather | solution.py:102
  269.5 2.0 convolution_convert_fusion
  271.6 3.8 fusion.57
  275.4 8.1 %fusion.11 = f32[2,64,4096]{2,1,0:T(8,128)} fusion(bf16[2,384,4096]{2,1,0:T(8,128)(2,1)} %param.23, bf16[2,64,4096]{2,1,0:T(8,128)(2,1)S(1)} %convolution_convert_fusion, bf16[2,4096,384]{2,1,0:T(8,128)(2,1)} %param.22, f32[2,64,384]{2,1,0:T(8,128)S(1)} %fusion.57), kind=kOutput, calls=%fused_computation.12 | convolution fusion | flops 805601280 | bytes 15925248 | tf_op jit(solution)/shard_map/ecf,efd->ecd/dot_general | solution.py:74
  283.5 0.0 copy-start.1
  283.5 6.8 %convolution_bitcast_fusion = f32[256,4096]{1,0:T(8,128)} fusion(f32[2,64,4096]{2,1,0:T(8,128)} %fusion.11, f32[2,256]{1,0:T(2,128)S(1)} %bitcast.67, s32[2,256]{1,0:T(2,128)S(1)} %bitcast.60, pred[2,256]{1,0:T(4,128)(4,1)S(1)} %bitcast.64), kind=kOutput, calls=%fused_computation | convolution fusion | flops 1610711040 | bytes 6296064 | tf_op jit(solution)/shard_map/ecr,ecd->rd/dot_general | solution.py:107
  290.2 0.0 reduce-scatter.2.cloned.1.call-update
  290.3 0.0 all-reduce.5.cloned.1.call-start
  290.3 161.3 %reduce-scatter.2.cloned.1.call-done = f32[256,128]{1,0:T(8,128)} async-done(((f32[256,4096]{1,0:T(8,128)}), f32[256,128]{1,0:T(8,128)}) %reduce-scatter.2.cloned.1.call-update) | async-done | bytes 131088 | tf_op jit(solution)/shard_map/reduce_scatter | solution.py:108
  451.6 0.0 all-reduce.5.cloned.1.call-update
  451.7 62.3 %all-reduce.5.cloned.1.call-done = f32[256,128]{1,0:T(8,128)} async-done(((f32[256,128]{1,0:T(8,128)}), f32[256,128]{1,0:T(8,128)}) %all-reduce.5.cloned.1.call-update) | async-done | bytes 131088 | tf_op jit(solution)/shard_map/psum | solution.py:108
  514.0 0.0 copy-done.1
  514.0 1.6 add_convert_fusion
  (8 shorter events, 0.1 us)
Async XLA Ops:
  6.5 32.2 %copy-start = (bf16[2048,128]{1,0:T(8,128)(2,1)S(1)}, bf16[2048,128]{1,0:T(8,128)(2,1)}, u32[]{:S(2)}) copy-start(bf16[2048,128]{1,0:T(8,128)(2,1)} %param.17) | copy-start | bytes 1572868
  6.5 74.2 %all-reduce.3.cloned.1.call-start = ((), (), s32[]{:S(2)}) async-start(), calls=%async_computation.2 | async-start | bytes 262144 | tf_op jit(solution)/shard_map/psum | solution.py:99
  11.5 69.3 %copy-start.2 = (bf16[256,128]{1,0:T(8,128)(2,1)S(1)}, bf16[256,128]{1,0:T(8,128)(2,1)}, u32[]{:S(2)}) copy-start(bf16[256,128]{1,0:T(8,128)(2,1)} %param.16) | copy-start | bytes 196612
  11.5 138.3 %copy-start.5 = (f32[128]{0:T(128)S(1)}, f32[128]{0:T(128)}, u32[]{:S(2)}) copy-start(f32[128]{0:T(128)} %param.18) | copy-start | bytes 1540
  11.6 140.0 %copy-start.3 = (s32[256,8]{0,1:T(8,128)S(1)}, s32[256,8]{0,1:T(8,128)}, u32[]{:S(2)}) copy-start(s32[256,8]{0,1:T(8,128)} %param.19) | copy-start | bytes 24580
  11.6 141.2 %copy-start.4 = (f32[256,8]{0,1:T(8,128)S(1)}, f32[256,8]{0,1:T(8,128)}, u32[]{:S(2)}) copy-start(f32[256,8]{0,1:T(8,128)} %param.20) | copy-start | bytes 24580
  39.9 229.7 %all-gather.2.cloned.1.call-start = ((), (), s32[]{:S(2)}) async-start(), calls=%async_computation.3 | async-start | bytes 2162688 | tf_op jit(solution)/shard_map/all_gather | solution.py:102
  151.5 300.1 %reduce-scatter.2.cloned.1.call-start = ((), (), s32[]{:S(2)}) async-start(), calls=%async_computation.4 | async-start | bytes 4325376 | tf_op jit(solution)/shard_map/reduce_scatter | solution.py:108
  283.5 230.5 %copy-start.1 = (f32[256,128]{1,0:T(8,128)S(1)}, f32[256,128]{1,0:T(8,128)}, u32[]{:S(2)}) copy-start(f32[256,128]{1,0:T(8,128)} %all-reduce.3.cloned.1.call-done) | copy-start | bytes 393220
  290.3 223.7 %all-reduce.5.cloned.1.call-start = ((), (), s32[]{:S(2)}) async-start(), calls=%async_computation.5 | async-start | bytes 262144 | tf_op jit(solution)/shard_map/psum | solution.py:108
Sparse Core Ops, SparseCore 0:
  40.0 40.7 all-reduce.2
  151.6 117.8 all-gather.1
  290.4 161.2 reduce-scatter.1
  454.1 59.8 all-reduce.4
